TPU v7x, 32 devices: a whole 2x2x4 slice. The times are simulated.
32 devices in a mesh: dp: 16 (over z, y, x), mp: 2 (over core).
Axes of the slice: x: 2, y: 2, z: 4, core: 2. Of those that a mesh axis runs over, the one named last changes fastest.
Arguments:
- tokens: bfloat16 [36864, 768], P(('dp', 'mp')), may hold values from -6 to 6
- lengths: int32 [64], P('dp'), may hold values from 256 to 576, as said below
- gain_attn: float32 [768], replicated, may hold values from 0.5 to 1.5
- w_query: bfloat16 [768, 768], P(None, 'mp'), may hold values from -0.21875 to 0.21875
- w_key: bfloat16 [768, 768], P(None, 'mp'), may hold values from -0.21875 to 0.21875
- w_value: bfloat16 [768, 768], P(None, 'mp'), may hold values from -0.21875 to 0.21875
- w_out: bfloat16 [768, 768], P('mp'), may hold values from -1.75 to 1.75
- gain_ffn: float32 [768], replicated, may hold values from 0.5 to 1.5
- w_gate: bfloat16 [768, 2048], P(None, 'mp'), may hold values from -0.21875 to 0.21875
- w_up: bfloat16 [768, 2048], P(None, 'mp'), may hold values from -0.21875 to 0.21875
- w_down: bfloat16 [2048, 768], P('mp'), may hold values from -0.125 to 0.125
- cotangent: bfloat16 [36864, 768], P(('dp', 'mp')), may hold values from -6 to 6
Outputs:
- output: bfloat16 [36864, 768], P(('dp', 'mp'))
- grad_input: float32 [36864, 768], P(('dp', 'mp'))
- grad_gain_attn: float32 [768], replicated
- grad_query: float32 [768, 768], P('dp', 'mp')
- grad_key: float32 [768, 768], P('dp', 'mp')
- grad_value: float32 [768, 768], P('dp', 'mp')
- grad_out: float32 [768, 768], P('mp', 'dp')
- grad_gain_ffn: float32 [768], replicated
- grad_gate: float32 [768, 2048], P('dp', 'mp')
- grad_up: float32 [768, 2048], P('dp', 'mp')
- grad_down: float32 [2048, 768], P('mp', 'dp')
Inputs may be any that keep to these rules, and one draw needn't show every extreme that they name: `lengths`: each item's count of valid tokens, the class token first; exactly half of the 64 items have 576 and the other half 256.
All inputs are finite; a program needn't handle non-finite values.
Results may differ from a plain program's by a relative error of at most 0.013.
Values may be sent and summed in bfloat16 or wider, within the bound.
No kernel may reach another device: no remote copies, remote signals or barrier semaphores. Data moves between devices by JAX's collectives and lax.ppermute only.
A program may use at most 192 MiB of HBM per device.

v0:
```python
import jax
import jax.numpy as jnp
from jax import lax
from jax.sharding import PartitionSpec as P

HEAD = 64
SLOTS = 576
EPS = 1e-05
THETA = 10000.0


def tables(row_count):
    places = (jnp.arange(row_count) % SLOTS).astype(jnp.float32)
    inv_freq = THETA ** (-(2.0 * jnp.arange(HEAD // 2).astype(jnp.float32)) / HEAD)
    angles = places[:, None] * inv_freq[None, :]
    return (jnp.cos(angles), jnp.sin(angles))


def rotate(values, cosine, sine):
    half_width = values.shape[-1] // 2
    first_half = values[..., :half_width]
    second = values[..., half_width:]
    cos_b = cosine[:, None, :]
    sin_b = sine[:, None, :]
    return jnp.concatenate(
        [first_half * cos_b - second * sin_b, second * cos_b + first_half * sin_b], -1
    )


def unrotate(values, cosine, sine):
    half_width = values.shape[-1] // 2
    first_half = values[..., :half_width]
    second = values[..., half_width:]
    cos_b = cosine[:, None, :]
    sin_b = sine[:, None, :]
    return jnp.concatenate(
        [first_half * cos_b + second * sin_b, second * cos_b - first_half * sin_b], -1
    )


def contract_rows(left, right):
    return lax.dot_general(
        left, right, (((0,), (0,)), ((), ())), preferred_element_type=jnp.float32
    )


def contract_cols(left, right):
    return lax.dot_general(
        left, right, (((1,), (1,)), ((), ())), preferred_element_type=jnp.float32
    )


def norm_back(inputs, inv_rms, gain, d_normed):
    weighted = d_normed * gain
    d_inputs = inv_rms * weighted - inputs * inv_rms**3 * jnp.mean(
        weighted * inputs, -1, keepdims=True
    )
    d_gain = jnp.sum(d_normed * inputs * inv_rms, 0)
    return (d_inputs, d_gain)


def local(
    tokens,
    lengths,
    gain_attn,
    w_query,
    w_key,
    w_value,
    w_out,
    gain_ffn,
    w_gate,
    w_up,
    w_down,
    cotangent,
):
    half_rows = tokens.shape[0]
    score_scale = HEAD ** (-0.5)
    q_weight, k_weight, v_weight, o_weight = (w_query, w_key, w_value, w_out)
    g_weight, u_weight, d_weight = (w_gate, w_up, w_down)
    local_cols = q_weight.shape[1]
    head_count = local_cols // HEAD
    resid_in = tokens.astype(jnp.float32)
    inv_rms_a = lax.rsqrt(jnp.mean(resid_in * resid_in, -1, keepdims=True) + EPS)
    normed_a = (resid_in * inv_rms_a * gain_attn).astype(jnp.bfloat16)
    gathered_a = lax.all_gather(normed_a, "mp", axis=0, tiled=True)
    all_rows = gathered_a.shape[0]
    item_count = all_rows // SLOTS
    item_shape = (item_count, SLOTS, head_count, HEAD)
    cosine, sine = tables(all_rows)
    queries = rotate(
        jnp.dot(gathered_a, q_weight, preferred_element_type=jnp.float32).reshape(
            all_rows, head_count, HEAD
        ),
        cosine,
        sine,
    ).astype(jnp.bfloat16)
    key_heads = rotate(
        jnp.dot(gathered_a, k_weight, preferred_element_type=jnp.float32).reshape(
            all_rows, head_count, HEAD
        ),
        cosine,
        sine,
    ).astype(jnp.bfloat16)
    value_heads = jnp.dot(gathered_a, v_weight, preferred_element_type=jnp.float32).astype(
        jnp.bfloat16
    )
    q_items = queries.reshape(item_shape)
    k_items = key_heads.reshape(item_shape)
    v_items = value_heads.reshape(item_shape)
    places = jnp.arange(SLOTS)

    def masked_scores(q_item, k_item, length):
        scores = (
            jnp.einsum("qhd,khd->hqk", q_item, k_item, preferred_element_type=jnp.float32)
            * score_scale
        )
        allowed = (places[None, :] <= places[:, None]) & (places[None, :] < length)
        return jnp.where(allowed[None], scores, -1e30)

    def attend(item_args):
        q_item, k_item, v_item, length = item_args
        scores = masked_scores(q_item, k_item, length)
        top_score = jnp.max(scores, -1, keepdims=True)
        expo = jnp.exp(scores - top_score)
        total = jnp.sum(expo, -1, keepdims=True)
        soft_probs = (expo / total).astype(jnp.bfloat16)
        mixed_item = jnp.einsum(
            "hqk,khd->qhd", soft_probs, v_item, preferred_element_type=jnp.float32
        )
        return (mixed_item.astype(jnp.bfloat16), (top_score + jnp.log(total))[..., 0])

    mixed_heads, log_norm = lax.map(attend, (q_items, k_items, v_items, lengths))
    attn_rows = mixed_heads.reshape(all_rows, local_cols)
    attn_branch = lax.psum_scatter(
        jnp.dot(attn_rows, o_weight, preferred_element_type=jnp.float32),
        "mp",
        scatter_dimension=0,
        tiled=True,
    )
    middle = resid_in + attn_branch
    inv_rms_f = lax.rsqrt(jnp.mean(middle * middle, -1, keepdims=True) + EPS)
    normed_f = (middle * inv_rms_f * gain_ffn).astype(jnp.bfloat16)
    gathered_f = lax.all_gather(normed_f, "mp", axis=0, tiled=True)
    gate_pre = jnp.dot(gathered_f, g_weight, preferred_element_type=jnp.float32)
    up_pre = jnp.dot(gathered_f, u_weight, preferred_element_type=jnp.float32)
    sigmoid_g = jax.nn.sigmoid(gate_pre)
    silu_g = gate_pre * sigmoid_g
    hidden = (silu_g * up_pre).astype(jnp.bfloat16)
    ffn_branch = lax.psum_scatter(
        jnp.dot(hidden, d_weight, preferred_element_type=jnp.float32).astype(jnp.bfloat16),
        "mp",
        scatter_dimension=0,
        tiled=True,
    ).astype(jnp.float32)
    row_index = lax.axis_index("mp") * half_rows + jnp.arange(half_rows)
    final_rows = middle + ffn_branch
    owner = (row_index // SLOTS)[:, None] == jnp.arange(item_count)[None, :]
    limit = jnp.sum(jnp.where(owner, lengths[None, :], 0), 1)
    valid_rows = (row_index % SLOTS < limit).astype(jnp.float32)[:, None]
    output = (valid_rows * final_rows).astype(jnp.bfloat16)
    d_final = valid_rows * cotangent.astype(jnp.float32)
    d_ffn_all = lax.all_gather(d_final.astype(jnp.bfloat16), "mp", axis=0, tiled=True)
    grad_down = contract_rows(hidden, d_ffn_all)
    d_hidden = contract_cols(d_ffn_all, d_weight)
    d_gate = (d_hidden * up_pre * (sigmoid_g * (1.0 + gate_pre * (1.0 - sigmoid_g)))).astype(
        jnp.bfloat16
    )
    d_up = (d_hidden * silu_g).astype(jnp.bfloat16)
    grad_gate = contract_rows(gathered_f, d_gate)
    grad_up = contract_rows(gathered_f, d_up)
    ffn_sums = (
        lax.psum_scatter(grad_gate, "dp", scatter_dimension=0, tiled=True),
        lax.psum_scatter(grad_up, "dp", scatter_dimension=0, tiled=True),
        lax.psum_scatter(grad_down, "dp", scatter_dimension=1, tiled=True),
    )
    d_normed_f = lax.psum_scatter(
        contract_cols(d_gate, g_weight) + contract_cols(d_up, u_weight),
        "mp",
        scatter_dimension=0,
        tiled=True,
    )
    d_middle_norm, d_gain_ffn = norm_back(middle, inv_rms_f, gain_ffn, d_normed_f)
    d_middle = d_final + d_middle_norm
    d_attn_all = lax.all_gather(d_middle.astype(jnp.bfloat16), "mp", axis=0, tiled=True)
    grad_out = contract_rows(attn_rows, d_attn_all)
    d_mixed = contract_cols(d_attn_all, o_weight).astype(jnp.bfloat16).reshape(item_shape)

    def attend_back(item_args):
        q_item, k_item, v_item, length, norm_item, d_item = item_args
        scores = masked_scores(q_item, k_item, length)
        soft_probs = jnp.exp(scores - norm_item[..., None])
        d_value = jnp.einsum(
            "hqk,qhd->khd",
            soft_probs.astype(jnp.bfloat16),
            d_item,
            preferred_element_type=jnp.float32,
        )
        d_soft = jnp.einsum("qhd,khd->hqk", d_item, v_item, preferred_element_type=jnp.float32)
        d_scores = (soft_probs * (d_soft - jnp.sum(soft_probs * d_soft, -1, keepdims=True))).astype(
            jnp.bfloat16
        )
        d_query = (
            jnp.einsum("hqk,khd->qhd", d_scores, k_item, preferred_element_type=jnp.float32)
            * score_scale
        )
        d_key = (
            jnp.einsum("hqk,qhd->khd", d_scores, q_item, preferred_element_type=jnp.float32)
            * score_scale
        )
        return (d_query, d_key, d_value)

    d_queries, d_keys, d_values = lax.map(
        attend_back, (q_items, k_items, v_items, lengths, log_norm, d_mixed)
    )
    d_q_rows = (
        unrotate(d_queries.reshape(all_rows, head_count, HEAD), cosine, sine)
        .astype(jnp.bfloat16)
        .reshape(all_rows, local_cols)
    )
    d_k_rows = (
        unrotate(d_keys.reshape(all_rows, head_count, HEAD), cosine, sine)
        .astype(jnp.bfloat16)
        .reshape(all_rows, local_cols)
    )
    d_v_rows = d_values.astype(jnp.bfloat16).reshape(all_rows, local_cols)
    grad_query = contract_rows(gathered_a, d_q_rows)
    grad_key = contract_rows(gathered_a, d_k_rows)
    grad_value = contract_rows(gathered_a, d_v_rows)
    d_normed_a = lax.psum_scatter(
        contract_cols(d_q_rows, q_weight)
        + contract_cols(d_k_rows, k_weight)
        + contract_cols(d_v_rows, v_weight),
        "mp",
        scatter_dimension=0,
        tiled=True,
    )
    d_input_norm, d_gain_attn = norm_back(resid_in, inv_rms_a, gain_attn, d_normed_a)
    grad_input = d_middle + d_input_norm
    gain_grads = lax.psum((d_gain_attn, d_gain_ffn), ("dp", "mp"))
    attn_sums = (
        lax.psum_scatter(grad_query, "dp", scatter_dimension=0, tiled=True),
        lax.psum_scatter(grad_key, "dp", scatter_dimension=0, tiled=True),
        lax.psum_scatter(grad_value, "dp", scatter_dimension=0, tiled=True),
        lax.psum_scatter(grad_out, "dp", scatter_dimension=1, tiled=True),
    )
    summed = (
        attn_sums[0],
        attn_sums[1],
        attn_sums[2],
        attn_sums[3],
        ffn_sums[0],
        ffn_sums[1],
        ffn_sums[2],
    )
    return (
        output,
        grad_input,
        gain_grads[0],
        summed[0],
        summed[1],
        summed[2],
        summed[3],
        gain_grads[1],
        summed[4],
        summed[5],
        summed[6],
    )


def solution(mesh):
    in_specs = (
        P(("dp", "mp"), None),
        P("dp"),
        P(),
        P(None, "mp"),
        P(None, "mp"),
        P(None, "mp"),
        P("mp", None),
        P(),
        P(None, "mp"),
        P(None, "mp"),
        P("mp", None),
        P(("dp", "mp"), None),
    )
    out_specs = (
        P(("dp", "mp"), None),
        P(("dp", "mp"), None),
        P(),
        P("dp", "mp"),
        P("dp", "mp"),
        P("dp", "mp"),
        P("mp", "dp"),
        P(),
        P("dp", "mp"),
        P("dp", "mp"),
        P("mp", "dp"),
    )
    return jax.shard_map(local, mesh=mesh, in_specs=in_specs, out_specs=out_specs, check_vma=False)
```

profile of v0, /device:TPU:0, one launch (start us, length us, event | category | flops | bytes accessed | tf_op | source)
XLA Modules:
  0.0 1483.8 jit_solution(9570107461674244627)
XLA Ops:
  15.7 13.5 all-gather.5.cloned.1.call-done
  63.9 42.3 %while.30 = (s32[]{:T(128)}, bf16[4,576,6,64]{1,3,2,0:T(8,128)(2,1)S(1)}, f32[4,6,576]{2,1,0:T(8,128)}, bf16[4,576,6,64]{1,3,2,0:T(8,128)(2,1)}, s32[4]{0:T(128)...) while((s32[]{:T(128)}, ...), condition=%wide.region_5.6_spmd.clone.clone, body=%wide.region_2.5_spmd.clone.clone.sunk | while | flops 534377664 | bytes 28236528 | solution.py:132
  112.5 6.4 fusion.83
  119.0 16.7 %reduce-scatter.12.cloned.1.call-done = f32[1152,768]{1,0:T(8,128)} async-done(((f32[2304,768]{1,0:T(8,128)}), f32[1152,768]{1,0:T(8,128)}) %reduce-scatter.12.cloned.1.call-update) | async-done | bytes 3538960 | tf_op jit(solution)/shard_map/reduce_scatter | solution.py:134
  143.7 11.9 all-gather.7.cloned.1.call-done
  155.6 10.5 fusion.85
  172.4 14.8 multiply_convert_fusion.1
  187.2 7.5 fusion.86
  201.1 7.7 convolution_convert_fusion
  208.8 8.7 reduce-scatter.16.cloned.1.call-done
  221.6 10.8 reduce-scatter.14.cloned.1.call-done
  238.3 13.9 all-gather.11.cloned.1.call-done
  264.7 246.6 %while.31 = (s32[]{:T(128)}, f32[4,576,6,64]{1,0,3,2:T(4,128)}, f32[4,576,6,64]{1,0,3,2:T(4,128)}, bf16[4,576,6,64]{1,3,2,0:T(8,128)(2,1)}, bf16[4,576,6,64]{1,3...) while((s32[]{:T(128)}, f32[4,576,6,64]{1,0,3,2:T(4,128)}, ...), condition=%wide.region_13.14_spmd.clone.clone, body=%wide.region_11.13_spmd.clone.clone.sunk | while | flops 1304982784 | bytes 89503072 | solution.py:212
  287.4 19.6 %dynamic_update_slice.40 = f32[4,576,6,64]{1,0,3,2:T(4,128)} dynamic-update-slice(f32[4,576,6,64]{1,0,3,2:T(4,128)} %get-tuple-element.481, f32[1,576,6,64]{1,0,3,2:T(1,128)S(1)} %copy.81, s32[]{:T(128)S(6)} %copy.100, s32[]{:T(128)} %constant.88.clone.1..sunk, s32[]{:T(128)} %constant.88.clone.1..sunk, s32[]{:T(128)} %constant.88.clone.1..sunk) | dynamic-update-slice | bytes 1769476 | tf_op jit(solution)/shard_map/while/body/jit(dynamic_update_index_in_dim)/dynamic_update_slice | solution.py:212
  307.1 19.6 %dynamic_update_slice.39 = f32[4,576,6,64]{1,0,3,2:T(4,128)} dynamic-update-slice(f32[4,576,6,64]{1,0,3,2:T(4,128)} %get-tuple-element.480, f32[1,576,6,64]{1,0,3,2:T(1,128)S(1)} %copy.80, s32[]{:T(128)S(6)} %copy.100, s32[]{:T(128)} %constant.88.clone.1..sunk, s32[]{:T(128)} %constant.88.clone.1..sunk, s32[]{:T(128)} %constant.88.clone.1..sunk) | dynamic-update-slice | bytes 1769476 | tf_op jit(solution)/shard_map/while/body/jit(dynamic_update_index_in_dim)/dynamic_update_slice | solution.py:212
  348.9 19.6 %dynamic_update_slice.40 = f32[4,576,6,64]{1,0,3,2:T(4,128)} dynamic-update-slice(f32[4,576,6,64]{1,0,3,2:T(4,128)} %get-tuple-element.481, f32[1,576,6,64]{1,0,3,2:T(1,128)S(1)} %copy.81, s32[]{:T(128)S(6)} %copy.100, s32[]{:T(128)} %constant.88.clone.1..sunk, s32[]{:T(128)} %constant.88.clone.1..sunk, s32[]{:T(128)} %constant.88.clone.1..sunk) | dynamic-update-slice | bytes 1769476 | tf_op jit(solution)/shard_map/while/body/jit(dynamic_update_index_in_dim)/dynamic_update_slice | solution.py:212
  368.6 19.6 %dynamic_update_slice.39 = f32[4,576,6,64]{1,0,3,2:T(4,128)} dynamic-update-slice(f32[4,576,6,64]{1,0,3,2:T(4,128)} %get-tuple-element.480, f32[1,576,6,64]{1,0,3,2:T(1,128)S(1)} %copy.80, s32[]{:T(128)S(6)} %copy.100, s32[]{:T(128)} %constant.88.clone.1..sunk, s32[]{:T(128)} %constant.88.clone.1..sunk, s32[]{:T(128)} %constant.88.clone.1..sunk) | dynamic-update-slice | bytes 1769476 | tf_op jit(solution)/shard_map/while/body/jit(dynamic_update_index_in_dim)/dynamic_update_slice | solution.py:212
  410.4 19.6 %dynamic_update_slice.40 = f32[4,576,6,64]{1,0,3,2:T(4,128)} dynamic-update-slice(f32[4,576,6,64]{1,0,3,2:T(4,128)} %get-tuple-element.481, f32[1,576,6,64]{1,0,3,2:T(1,128)S(1)} %copy.81, s32[]{:T(128)S(6)} %copy.100, s32[]{:T(128)} %constant.88.clone.1..sunk, s32[]{:T(128)} %constant.88.clone.1..sunk, s32[]{:T(128)} %constant.88.clone.1..sunk) | dynamic-update-slice | bytes 1769476 | tf_op jit(solution)/shard_map/while/body/jit(dynamic_update_index_in_dim)/dynamic_update_slice | solution.py:212
  430.1 19.6 %dynamic_update_slice.39 = f32[4,576,6,64]{1,0,3,2:T(4,128)} dynamic-update-slice(f32[4,576,6,64]{1,0,3,2:T(4,128)} %get-tuple-element.480, f32[1,576,6,64]{1,0,3,2:T(1,128)S(1)} %copy.80, s32[]{:T(128)S(6)} %copy.100, s32[]{:T(128)} %constant.88.clone.1..sunk, s32[]{:T(128)} %constant.88.clone.1..sunk, s32[]{:T(128)} %constant.88.clone.1..sunk) | dynamic-update-slice | bytes 1769476 | tf_op jit(solution)/shard_map/while/body/jit(dynamic_update_index_in_dim)/dynamic_update_slice | solution.py:212
  471.9 19.6 %dynamic_update_slice.40 = f32[4,576,6,64]{1,0,3,2:T(4,128)} dynamic-update-slice(f32[4,576,6,64]{1,0,3,2:T(4,128)} %get-tuple-element.481, f32[1,576,6,64]{1,0,3,2:T(1,128)S(1)} %copy.81, s32[]{:T(128)S(6)} %copy.100, s32[]{:T(128)} %constant.88.clone.1..sunk, s32[]{:T(128)} %constant.88.clone.1..sunk, s32[]{:T(128)} %constant.88.clone.1..sunk) | dynamic-update-slice | bytes 1769476 | tf_op jit(solution)/shard_map/while/body/jit(dynamic_update_index_in_dim)/dynamic_update_slice | solution.py:212
  491.6 19.6 %dynamic_update_slice.39 = f32[4,576,6,64]{1,0,3,2:T(4,128)} dynamic-update-slice(f32[4,576,6,64]{1,0,3,2:T(4,128)} %get-tuple-element.480, f32[1,576,6,64]{1,0,3,2:T(1,128)S(1)} %copy.80, s32[]{:T(128)S(6)} %copy.100, s32[]{:T(128)} %constant.88.clone.1..sunk, s32[]{:T(128)} %constant.88.clone.1..sunk, s32[]{:T(128)} %constant.88.clone.1..sunk) | dynamic-update-slice | bytes 1769476 | tf_op jit(solution)/shard_map/while/body/jit(dynamic_update_index_in_dim)/dynamic_update_slice | solution.py:212
  540.3 9.0 fusion.95
  549.4 10.8 fusion.93
  560.3 9.1 fusion.94
  595.1 40.7 %all-reduce = (f32[768]{0:T(1024)}, f32[768]{0:T(1024)}) all-reduce(f32[768]{0:T(1024)S(1)} %get-tuple-element.261, f32[768]{0:T(1024)S(1)} %copy-done.27), channel_id=1, replica_groups=mesh['dp'=16,'mp'=2] {'dp','mp'}, use_global_device_ids=true, to_apply=%region_17.18 | all-reduce | flops 1536 | bytes 12288 | tf_op jit(solution)/shard_map/psum | solution.py:239
  640.7 53.7 %reduce-scatter.32.cloned.1.call-done = f32[1024,48]{0,1:T(8,128)} async-done(((f32[1024,768]{0,1:T(8,128)}), f32[1024,48]{0,1:T(8,128)}) %reduce-scatter.32.cloned.1.call-update) | async-done | bytes 196624 | tf_op jit(solution)/shard_map/reduce_scatter | solution.py:174
  694.4 135.5 %reduce-scatter.28.cloned.1.call-done = f32[48,1024]{1,0:T(8,128)} async-done(((f32[768,1024]{1,0:T(8,128)}), f32[48,1024]{1,0:T(8,128)}) %reduce-scatter.28.cloned.1.call-update) | async-done | bytes 196624 | tf_op jit(solution)/shard_map/reduce_scatter | solution.py:172
  829.8 135.5 %reduce-scatter.30.cloned.1.call-done = f32[48,1024]{1,0:T(8,128)} async-done(((f32[768,1024]{1,0:T(8,128)}), f32[48,1024]{1,0:T(8,128)}) %reduce-scatter.30.cloned.1.call-update) | async-done | bytes 196624 | tf_op jit(solution)/shard_map/reduce_scatter | solution.py:173
  965.4 128.0 %reduce-scatter.26.cloned.1.call-done = f32[384,48]{0,1:T(8,128)} async-done(((f32[384,768]{0,1:T(8,128)}), f32[384,48]{0,1:T(8,128)}) %reduce-scatter.26.cloned.1.call-update) | async-done | bytes 73744 | tf_op jit(solution)/shard_map/reduce_scatter | solution.py:244
  1093.4 128.0 %reduce-scatter.24.cloned.1.call-done = f32[48,384]{1,0:T(8,128)} async-done(((f32[768,384]{1,0:T(8,128)}), f32[48,384]{1,0:T(8,128)}) %reduce-scatter.24.cloned.1.call-update) | async-done | bytes 73744 | tf_op jit(solution)/shard_map/reduce_scatter | solution.py:243
  1221.4 127.7 %reduce-scatter.20.cloned.1.call-done = f32[48,384]{1,0:T(8,128)} async-done(((f32[768,384]{1,0:T(8,128)}), f32[48,384]{1,0:T(8,128)}) %reduce-scatter.20.cloned.1.call-update) | async-done | bytes 73744 | tf_op jit(solution)/shard_map/reduce_scatter | solution.py:241
  1349.1 127.7 %reduce-scatter.22.cloned.1.call-done = f32[48,384]{1,0:T(8,128)} async-done(((f32[768,384]{1,0:T(8,128)}), f32[48,384]{1,0:T(8,128)}) %reduce-scatter.22.cloned.1.call-update) | async-done | bytes 73744 | tf_op jit(solution)/shard_map/reduce_scatter | solution.py:242
  (250 shorter events, 282.9 us)
Async XLA Ops:
  7.2 165.2 %copy-start = (bf16[1024,768]{1,0:T(8,128)(2,1)S(1)}, bf16[1024,768]{1,0:T(8,128)(2,1)}, u32[]{:S(2)}) copy-start(bf16[1024,768]{1,0:T(8,128)(2,1)} %param.26) | copy-start | bytes 4718596
  7.2 22.0 %all-gather.5.cloned.1.call-start = ((), (), s32[]{:S(2)}) async-start(), calls=%async_computation.11 | async-start | bytes 5308416 | tf_op jit(solution)/shard_map/all_gather | solution.py:85
  13.6 122.1 %reduce-scatter.12.cloned.1.call-start = ((), (), s32[]{:S(2)}) async-start(), calls=%async_computation.12 | async-start | bytes 10616832 | tf_op jit(solution)/shard_map/reduce_scatter | solution.py:134
  112.5 6.4 copy-start.6
  118.9 16.8 %copy-start.4 = (bf16[1152,768]{1,0:T(8,128)(2,1)S(1)}, bf16[1152,768]{1,0:T(8,128)(2,1)}, u32[]{:S(2)}) copy-start(bf16[1152,768]{1,0:T(8,128)(2,1)} %param.16) | copy-start | bytes 5308420
  118.9 21.1 %copy-start.24 = (f32[768]{0:T(1024)S(1)}, f32[768]{0:T(1024)}, u32[]{:S(2)}) copy-start(f32[768]{0:T(1024)} %param.23) | copy-start | bytes 9220
  118.9 36.7 %all-gather.7.cloned.1.call-start = ((), (), s32[]{:S(2)}) async-start(), calls=%async_computation.13 | async-start | bytes 5308416 | tf_op jit(solution)/shard_map/all_gather | solution.py:143
  141.6 30.8 %all-gather.9.cloned.1.call-start = ((), (), s32[]{:S(2)}) async-start(), calls=%async_computation.15 | async-start | bytes 5308416 | tf_op jit(solution)/shard_map/all_gather | solution.py:162
  143.5 22.7 %copy-start.32 = (bf16[768,1024]{1,0:T(8,128)(2,1)S(1)}, bf16[768,1024]{1,0:T(8,128)(2,1)}, u32[]{:S(2)}) copy-start(bf16[768,1024]{1,0:T(8,128)(2,1)} %param.24) | copy-start | bytes 4718596
  143.5 74.0 %reduce-scatter.16.cloned.1.call-start = ((), (), s32[]{:S(2)}) async-start(), calls=%async_computation.16 | async-start | bytes 10616832 | tf_op jit(solution)/shard_map/reduce_scatter | solution.py:176
  155.6 10.5 copy-start.31
  187.2 7.5 copy-start.34
  187.2 7.5 copy-start.33
  200.8 31.5 %reduce-scatter.14.cloned.1.call-start = ((), (), s32[]{:S(2)}) async-start(), calls=%async_computation.14 | async-start | bytes 5308416 | tf_op jit(solution)/shard_map/reduce_scatter | solution.py:149
  208.8 8.8 copy-start.3
  208.8 43.5 %all-gather.11.cloned.1.call-start = ((), (), s32[]{:S(2)}) async-start(), calls=%async_computation.17 | async-start | bytes 5308416 | tf_op jit(solution)/shard_map/all_gather | solution.py:184
  238.3 353.4 %reduce-scatter.18.cloned.1.call-start = ((), (), s32[]{:S(2)}) async-start(), calls=%async_computation.18 | async-start | bytes 10616832 | tf_op jit(solution)/shard_map/reduce_scatter | solution.py:229
  258.8 6.0 copy-start.29
  273.5 5.0 copy-start.16
  540.0 154.3 %reduce-scatter.32.cloned.1.call-start = ((), (), s32[]{:S(2)}) async-start(), calls=%async_computation.25 | async-start | bytes 3342336 | tf_op jit(solution)/shard_map/reduce_scatter | solution.py:174
  549.3 280.5 %reduce-scatter.28.cloned.1.call-start = ((), (), s32[]{:S(2)}) async-start(), calls=%async_computation.23 | async-start | bytes 3342336 | tf_op jit(solution)/shard_map/reduce_scatter | solution.py:172
  560.2 9.5 copy-start.7
  560.2 405.2 %reduce-scatter.30.cloned.1.call-start = ((), (), s32[]{:S(2)}) async-start(), calls=%async_computation.24 | async-start | bytes 3342336 | tf_op jit(solution)/shard_map/reduce_scatter | solution.py:173
  569.3 524.0 %reduce-scatter.26.cloned.1.call-start = ((), (), s32[]{:S(2)}) async-start(), calls=%async_computation.22 | async-start | bytes 1253376 | tf_op jit(solution)/shard_map/reduce_scatter | solution.py:244
  574.8 646.5 %reduce-scatter.24.cloned.1.call-start = ((), (), s32[]{:S(2)}) async-start(), calls=%async_computation.21 | async-start | bytes 1253376 | tf_op jit(solution)/shard_map/reduce_scatter | solution.py:243
  580.5 768.6 %reduce-scatter.20.cloned.1.call-start = ((), (), s32[]{:S(2)}) async-start(), calls=%async_computation.19 | async-start | bytes 1253376 | tf_op jit(solution)/shard_map/reduce_scatter | solution.py:241
  585.7 5.9 copy-start.5
  585.7 5.9 copy-start.23
  585.7 5.9 copy-start.25
  585.7 891.1 %reduce-scatter.22.cloned.1.call-start = ((), (), s32[]{:S(2)}) async-start(), calls=%async_computation.20 | async-start | bytes 1253376 | tf_op jit(solution)/shard_map/reduce_scatter | solution.py:242
  591.6 44.2 %copy-start.26 = (f32[1152]{0:T(1024)S(1)}, f32[1152]{0:T(1024)}, u32[]{:S(2)}) copy-start(f32[1152]{0:T(1024)} %get-tuple-element.325) | copy-start | bytes 13828
  635.7 841.1 %copy-start.1 = (bf16[1024,768]{1,0:T(8,128)(2,1)S(1)}, bf16[1024,768]{1,0:T(8,128)(2,1)}, u32[]{:S(2)}) copy-start(bf16[1024,768]{1,0:T(8,128)(2,1)} %param.26) | copy-start | bytes 4718596
  (24 other events, 63.0 us)
Sparse Core Ops, SparseCore 0:
  13.7 15.3 all-gather.4
  119.0 16.6 reduce-scatter.11
  141.8 13.8 all-gather.6
  157.1 13.8 all-gather.8
  200.9 16.5 reduce-scatter.15
  219.6 12.6 reduce-scatter.13
  238.4 13.8 all-gather.10
  540.2 16.6 reduce-scatter.17
  562.4 131.9 reduce-scatter.31
  699.8 130.0 reduce-scatter.27
  835.4 129.9 reduce-scatter.29
  970.5 122.7 reduce-scatter.25
  1098.7 122.5 reduce-scatter.23
  1226.5 122.5 reduce-scatter.19
  1354.3 122.5 reduce-scatter.21
where the time goes:
time: 1500 us; the launch traced here: 1480 us
  waiting for transfers between devices  912 us (61%)
  local copies, waits for them, and re-layouts  225 us (15%)
  matrix products  221 us (15%)
  other arithmetic  67.5 us (4%)
  blocking collectives  40.7 us (3%)
    dynamic_update_slice x16, local copies, waits for them, and re-layouts, local(): lax.map(attend_back, (q_items, k_items, v_items, lengths, log_norm, d_mix...  165 us
    reduce_scatter x1, waiting for transfers between devices, local(): lax.psum_scatter(grad_up, 'dp', scatter_dimension=0, tiled=True)  136 us
    reduce_scatter x1, waiting for transfers between devices, local(): lax.psum_scatter(grad_gate, 'dp', scatter_dimension=0, tiled=True)  135 us
    reduce_scatter x1, waiting for transfers between devices, local(): lax.psum_scatter(grad_out, 'dp', scatter_dimension=1, tiled=True)  128 us
    reduce_scatter x1, waiting for transfers between devices, local(): lax.psum_scatter(grad_value, 'dp', scatter_dimension=0, tiled=True)  128 us
    reduce_scatter x1, waiting for transfers between devices, local(): lax.psum_scatter(grad_query, 'dp', scatter_dimension=0, tiled=True)  128 us
    reduce_scatter x1, waiting for transfers between devices, local(): lax.psum_scatter(grad_key, 'dp', scatter_dimension=0, tiled=True)  128 us
    reduce_scatter x1, waiting for transfers between devices, local(): lax.psum_scatter(grad_down, 'dp', scatter_dimension=1, tiled=True)  53.7 us
  transfers between devices with their start and end apart: 15, of which 13 were waited for; matrix products, arithmetic and copies ran while one was open for 6% of the time, Pallas kernels for 0%

commit v1 on v0

--- a/solution.py
+++ b/solution.py
@@ -236,7 +236,7 @@
     )
     d_input_norm, d_gain_attn = norm_back(resid_in, inv_rms_a, gain_attn, d_normed_a)
     grad_input = d_middle + d_input_norm
-    gain_grads = lax.psum((d_gain_attn, d_gain_ffn), ("dp", "mp"))
+    gain_grads = lax.psum(lax.psum((d_gain_attn, d_gain_ffn), "dp"), "mp")
     attn_sums = (
         lax.psum_scatter(grad_query, "dp", scatter_dimension=0, tiled=True),
         lax.psum_scatter(grad_key, "dp", scatter_dimension=0, tiled=True),

time: 1500 us -> 1500 us (level)
    psum x1 -> x2, blocking collectives: 40.7 us -> 46.1 us  [local(): gain_grads = lax.psum(lax.psum((d_gain_attn, d_gain_ffn), 'dp'), 'mp')]
where the time goes in v1:
time: 1500 us; the launch traced here: 1480 us
  waiting for transfers between devices  906 us (60%)
  local copies, waits for them, and re-layouts  225 us (15%)
  matrix products  221 us (15%)
  other arithmetic  67.5 us (4%)
  blocking collectives  46.1 us (3%)
    dynamic_update_slice x16, local copies, waits for them, and re-layouts, local(): lax.map(attend_back, (q_items, k_items, v_items, lengths, log_norm, d_mix...  165 us
    reduce_scatter x1, waiting for transfers between devices, local(): lax.psum_scatter(grad_up, 'dp', scatter_dimension=0, tiled=True)  136 us
    reduce_scatter x1, waiting for transfers between devices, local(): lax.psum_scatter(grad_gate, 'dp', scatter_dimension=0, tiled=True)  135 us
    reduce_scatter x1, waiting for transfers between devices, local(): lax.psum_scatter(grad_out, 'dp', scatter_dimension=1, tiled=True)  128 us
    reduce_scatter x1, waiting for transfers between devices, local(): lax.psum_scatter(grad_value, 'dp', scatter_dimension=0, tiled=True)  128 us
    reduce_scatter x1, waiting for transfers between devices, local(): lax.psum_scatter(grad_query, 'dp', scatter_dimension=0, tiled=True)  128 us
    reduce_scatter x1, waiting for transfers between devices, local(): lax.psum_scatter(grad_key, 'dp', scatter_dimension=0, tiled=True)  128 us
    dot_general x7, matrix products, contract_rows(): lax.dot_general(left, right, (((0,), (0,)), ((), ())), preferred_element_...  50.5 us
  transfers between devices with their start and end apart: 15, of which 13 were waited for; matrix products, arithmetic and copies ran while one was open for 6% of the time, Pallas kernels for 0%

profile of v1, /device:TPU:0, one launch (start us, length us, event | category | flops | bytes accessed | tf_op | source)
XLA Modules:
  0.0 1483.8 jit_solution(17902074403007894805)
XLA Ops:
  15.6 13.5 all-gather.5.cloned.1.call-done
  63.8 42.3 %while.30 = (s32[]{:T(128)}, bf16[4,576,6,64]{1,3,2,0:T(8,128)(2,1)S(1)}, f32[4,6,576]{2,1,0:T(8,128)}, bf16[4,576,6,64]{1,3,2,0:T(8,128)(2,1)}, s32[4]{0:T(128)...) while((s32[]{:T(128)}, ...), condition=%wide.region_5.6_spmd.clone.clone, body=%wide.region_2.5_spmd.clone.clone.sunk | while | flops 534377664 | bytes 28236528 | solution.py:132
  112.5 6.4 fusion.83
  118.9 16.7 %reduce-scatter.12.cloned.1.call-done = f32[1152,768]{1,0:T(8,128)} async-done(((f32[2304,768]{1,0:T(8,128)}), f32[1152,768]{1,0:T(8,128)}) %reduce-scatter.12.cloned.1.call-update) | async-done | bytes 3538960 | tf_op jit(solution)/shard_map/reduce_scatter | solution.py:134
  143.7 11.9 all-gather.7.cloned.1.call-done
  155.6 10.5 fusion.85
  172.4 14.8 multiply_convert_fusion.1
  187.2 7.5 fusion.86
  201.0 7.7 convolution_convert_fusion
  208.8 8.7 reduce-scatter.16.cloned.1.call-done
  221.5 10.8 reduce-scatter.14.cloned.1.call-done
  238.3 13.9 all-gather.11.cloned.1.call-done
  264.7 246.6 %while.31 = (s32[]{:T(128)}, f32[4,576,6,64]{1,0,3,2:T(4,128)}, f32[4,576,6,64]{1,0,3,2:T(4,128)}, bf16[4,576,6,64]{1,3,2,0:T(8,128)(2,1)}, bf16[4,576,6,64]{1,3...) while((s32[]{:T(128)}, f32[4,576,6,64]{1,0,3,2:T(4,128)}, ...), condition=%wide.region_13.14_spmd.clone.clone, body=%wide.region_11.13_spmd.clone.clone.sunk | while | flops 1304982784 | bytes 89503072 | solution.py:212
  287.4 19.6 %dynamic_update_slice.40 = f32[4,576,6,64]{1,0,3,2:T(4,128)} dynamic-update-slice(f32[4,576,6,64]{1,0,3,2:T(4,128)} %get-tuple-element.483, f32[1,576,6,64]{1,0,3,2:T(1,128)S(1)} %copy.81, s32[]{:T(128)S(6)} %copy.100, s32[]{:T(128)} %constant.88.clone.1..sunk, s32[]{:T(128)} %constant.88.clone.1..sunk, s32[]{:T(128)} %constant.88.clone.1..sunk) | dynamic-update-slice | bytes 1769476 | tf_op jit(solution)/shard_map/while/body/jit(dynamic_update_index_in_dim)/dynamic_update_slice | solution.py:212
  307.0 19.6 %dynamic_update_slice.39 = f32[4,576,6,64]{1,0,3,2:T(4,128)} dynamic-update-slice(f32[4,576,6,64]{1,0,3,2:T(4,128)} %get-tuple-element.482, f32[1,576,6,64]{1,0,3,2:T(1,128)S(1)} %copy.80, s32[]{:T(128)S(6)} %copy.100, s32[]{:T(128)} %constant.88.clone.1..sunk, s32[]{:T(128)} %constant.88.clone.1..sunk, s32[]{:T(128)} %constant.88.clone.1..sunk) | dynamic-update-slice | bytes 1769476 | tf_op jit(solution)/shard_map/while/body/jit(dynamic_update_index_in_dim)/dynamic_update_slice | solution.py:212
  348.9 19.6 %dynamic_update_slice.40 = f32[4,576,6,64]{1,0,3,2:T(4,128)} dynamic-update-slice(f32[4,576,6,64]{1,0,3,2:T(4,128)} %get-tuple-element.483, f32[1,576,6,64]{1,0,3,2:T(1,128)S(1)} %copy.81, s32[]{:T(128)S(6)} %copy.100, s32[]{:T(128)} %constant.88.clone.1..sunk, s32[]{:T(128)} %constant.88.clone.1..sunk, s32[]{:T(128)} %constant.88.clone.1..sunk) | dynamic-update-slice | bytes 1769476 | tf_op jit(solution)/shard_map/while/body/jit(dynamic_update_index_in_dim)/dynamic_update_slice | solution.py:212
  368.5 19.6 %dynamic_update_slice.39 = f32[4,576,6,64]{1,0,3,2:T(4,128)} dynamic-update-slice(f32[4,576,6,64]{1,0,3,2:T(4,128)} %get-tuple-element.482, f32[1,576,6,64]{1,0,3,2:T(1,128)S(1)} %copy.80, s32[]{:T(128)S(6)} %copy.100, s32[]{:T(128)} %constant.88.clone.1..sunk, s32[]{:T(128)} %constant.88.clone.1..sunk, s32[]{:T(128)} %constant.88.clone.1..sunk) | dynamic-update-slice | bytes 1769476 | tf_op jit(solution)/shard_map/while/body/jit(dynamic_update_index_in_dim)/dynamic_update_slice | solution.py:212
  410.4 19.6 %dynamic_update_slice.40 = f32[4,576,6,64]{1,0,3,2:T(4,128)} dynamic-update-slice(f32[4,576,6,64]{1,0,3,2:T(4,128)} %get-tuple-element.483, f32[1,576,6,64]{1,0,3,2:T(1,128)S(1)} %copy.81, s32[]{:T(128)S(6)} %copy.100, s32[]{:T(128)} %constant.88.clone.1..sunk, s32[]{:T(128)} %constant.88.clone.1..sunk, s32[]{:T(128)} %constant.88.clone.1..sunk) | dynamic-update-slice | bytes 1769476 | tf_op jit(solution)/shard_map/while/body/jit(dynamic_update_index_in_dim)/dynamic_update_slice | solution.py:212
  430.1 19.6 %dynamic_update_slice.39 = f32[4,576,6,64]{1,0,3,2:T(4,128)} dynamic-update-slice(f32[4,576,6,64]{1,0,3,2:T(4,128)} %get-tuple-element.482, f32[1,576,6,64]{1,0,3,2:T(1,128)S(1)} %copy.80, s32[]{:T(128)S(6)} %copy.100, s32[]{:T(128)} %constant.88.clone.1..sunk, s32[]{:T(128)} %constant.88.clone.1..sunk, s32[]{:T(128)} %constant.88.clone.1..sunk) | dynamic-update-slice | bytes 1769476 | tf_op jit(solution)/shard_map/while/body/jit(dynamic_update_index_in_dim)/dynamic_update_slice | solution.py:212
  472.0 19.6 %dynamic_update_slice.40 = f32[4,576,6,64]{1,0,3,2:T(4,128)} dynamic-update-slice(f32[4,576,6,64]{1,0,3,2:T(4,128)} %get-tuple-element.483, f32[1,576,6,64]{1,0,3,2:T(1,128)S(1)} %copy.81, s32[]{:T(128)S(6)} %copy.100, s32[]{:T(128)} %constant.88.clone.1..sunk, s32[]{:T(128)} %constant.88.clone.1..sunk, s32[]{:T(128)} %constant.88.clone.1..sunk) | dynamic-update-slice | bytes 1769476 | tf_op jit(solution)/shard_map/while/body/jit(dynamic_update_index_in_dim)/dynamic_update_slice | solution.py:212
  491.6 19.6 %dynamic_update_slice.39 = f32[4,576,6,64]{1,0,3,2:T(4,128)} dynamic-update-slice(f32[4,576,6,64]{1,0,3,2:T(4,128)} %get-tuple-element.482, f32[1,576,6,64]{1,0,3,2:T(1,128)S(1)} %copy.80, s32[]{:T(128)S(6)} %copy.100, s32[]{:T(128)} %constant.88.clone.1..sunk, s32[]{:T(128)} %constant.88.clone.1..sunk, s32[]{:T(128)} %constant.88.clone.1..sunk) | dynamic-update-slice | bytes 1769476 | tf_op jit(solution)/shard_map/while/body/jit(dynamic_update_index_in_dim)/dynamic_update_slice | solution.py:212
  540.3 9.0 fusion.95
  549.4 10.8 fusion.93
  560.2 9.1 fusion.94
  595.0 43.0 %all-reduce = (f32[768]{0:T(1024)S(1)}, f32[768]{0:T(1024)S(1)}) all-reduce(f32[768]{0:T(1024)S(1)} %get-tuple-element.261, f32[768]{0:T(1024)S(1)} %copy-done.27), channel_id=1, replica_groups=mesh['dp'=16,'mp'=2] {'dp'}, use_global_device_ids=true, to_apply=%region_17.18 | all-reduce | flops 1536 | bytes 12288 | tf_op jit(solution)/shard_map/psum | solution.py:239
  646.1 48.3 %reduce-scatter.32.cloned.1.call-done = f32[1024,48]{0,1:T(8,128)} async-done(((f32[1024,768]{0,1:T(8,128)}), f32[1024,48]{0,1:T(8,128)}) %reduce-scatter.32.cloned.1.call-update) | async-done | bytes 196624 | tf_op jit(solution)/shard_map/reduce_scatter | solution.py:174
  694.4 135.4 %reduce-scatter.28.cloned.1.call-done = f32[48,1024]{1,0:T(8,128)} async-done(((f32[768,1024]{1,0:T(8,128)}), f32[48,1024]{1,0:T(8,128)}) %reduce-scatter.28.cloned.1.call-update) | async-done | bytes 196624 | tf_op jit(solution)/shard_map/reduce_scatter | solution.py:172
  829.8 135.6 %reduce-scatter.30.cloned.1.call-done = f32[48,1024]{1,0:T(8,128)} async-done(((f32[768,1024]{1,0:T(8,128)}), f32[48,1024]{1,0:T(8,128)}) %reduce-scatter.30.cloned.1.call-update) | async-done | bytes 196624 | tf_op jit(solution)/shard_map/reduce_scatter | solution.py:173
  965.4 128.0 %reduce-scatter.26.cloned.1.call-done = f32[384,48]{0,1:T(8,128)} async-done(((f32[384,768]{0,1:T(8,128)}), f32[384,48]{0,1:T(8,128)}) %reduce-scatter.26.cloned.1.call-update) | async-done | bytes 73744 | tf_op jit(solution)/shard_map/reduce_scatter | solution.py:244
  1093.4 127.9 %reduce-scatter.24.cloned.1.call-done = f32[48,384]{1,0:T(8,128)} async-done(((f32[768,384]{1,0:T(8,128)}), f32[48,384]{1,0:T(8,128)}) %reduce-scatter.24.cloned.1.call-update) | async-done | bytes 73744 | tf_op jit(solution)/shard_map/reduce_scatter | solution.py:243
  1221.2 127.8 %reduce-scatter.20.cloned.1.call-done = f32[48,384]{1,0:T(8,128)} async-done(((f32[768,384]{1,0:T(8,128)}), f32[48,384]{1,0:T(8,128)}) %reduce-scatter.20.cloned.1.call-update) | async-done | bytes 73744 | tf_op jit(solution)/shard_map/reduce_scatter | solution.py:241
  1349.0 127.8 %reduce-scatter.22.cloned.1.call-done = f32[48,384]{1,0:T(8,128)} async-done(((f32[768,384]{1,0:T(8,128)}), f32[48,384]{1,0:T(8,128)}) %reduce-scatter.22.cloned.1.call-update) | async-done | bytes 73744 | tf_op jit(solution)/shard_map/reduce_scatter | solution.py:242
  (251 shorter events, 286.0 us)
Async XLA Ops:
  7.2 165.2 %copy-start = (bf16[1024,768]{1,0:T(8,128)(2,1)S(1)}, bf16[1024,768]{1,0:T(8,128)(2,1)}, u32[]{:S(2)}) copy-start(bf16[1024,768]{1,0:T(8,128)(2,1)} %param.26) | copy-start | bytes 4718596
  7.2 22.0 %all-gather.5.cloned.1.call-start = ((), (), s32[]{:S(2)}) async-start(), calls=%async_computation.11 | async-start | bytes 5308416 | tf_op jit(solution)/shard_map/all_gather | solution.py:85
  13.6 122.0 %reduce-scatter.12.cloned.1.call-start = ((), (), s32[]{:S(2)}) async-start(), calls=%async_computation.12 | async-start | bytes 10616832 | tf_op jit(solution)/shard_map/reduce_scatter | solution.py:134
  112.4 6.4 copy-start.6
  118.9 16.8 %copy-start.4 = (bf16[1152,768]{1,0:T(8,128)(2,1)S(1)}, bf16[1152,768]{1,0:T(8,128)(2,1)}, u32[]{:S(2)}) copy-start(bf16[1152,768]{1,0:T(8,128)(2,1)} %param.16) | copy-start | bytes 5308420
  118.9 21.1 %copy-start.24 = (f32[768]{0:T(1024)S(1)}, f32[768]{0:T(1024)}, u32[]{:S(2)}) copy-start(f32[768]{0:T(1024)} %param.23) | copy-start | bytes 9220
  118.9 36.7 %all-gather.7.cloned.1.call-start = ((), (), s32[]{:S(2)}) async-start(), calls=%async_computation.13 | async-start | bytes 5308416 | tf_op jit(solution)/shard_map/all_gather | solution.py:143
  141.6 30.8 %all-gather.9.cloned.1.call-start = ((), (), s32[]{:S(2)}) async-start(), calls=%async_computation.15 | async-start | bytes 5308416 | tf_op jit(solution)/shard_map/all_gather | solution.py:162
  143.4 22.7 %copy-start.32 = (bf16[768,1024]{1,0:T(8,128)(2,1)S(1)}, bf16[768,1024]{1,0:T(8,128)(2,1)}, u32[]{:S(2)}) copy-start(bf16[768,1024]{1,0:T(8,128)(2,1)} %param.24) | copy-start | bytes 4718596
  143.5 74.0 %reduce-scatter.16.cloned.1.call-start = ((), (), s32[]{:S(2)}) async-start(), calls=%async_computation.16 | async-start | bytes 10616832 | tf_op jit(solution)/shard_map/reduce_scatter | solution.py:176
  155.6 10.5 copy-start.31
  187.1 7.5 copy-start.34
  187.1 7.5 copy-start.33
  200.8 31.5 %reduce-scatter.14.cloned.1.call-start = ((), (), s32[]{:S(2)}) async-start(), calls=%async_computation.14 | async-start | bytes 5308416 | tf_op jit(solution)/shard_map/reduce_scatter | solution.py:149
  208.7 8.8 copy-start.3
  208.7 43.5 %all-gather.11.cloned.1.call-start = ((), (), s32[]{:S(2)}) async-start(), calls=%async_computation.17 | async-start | bytes 5308416 | tf_op jit(solution)/shard_map/all_gather | solution.py:184
  238.2 353.4 %reduce-scatter.18.cloned.1.call-start = ((), (), s32[]{:S(2)}) async-start(), calls=%async_computation.18 | async-start | bytes 10616832 | tf_op jit(solution)/shard_map/reduce_scatter | solution.py:229
  258.8 6.0 copy-start.29
  335.0 5.0 copy-start.16
  540.1 154.3 %reduce-scatter.32.cloned.1.call-start = ((), (), s32[]{:S(2)}) async-start(), calls=%async_computation.25 | async-start | bytes 3342336 | tf_op jit(solution)/shard_map/reduce_scatter | solution.py:174
  549.3 280.5 %reduce-scatter.28.cloned.1.call-start = ((), (), s32[]{:S(2)}) async-start(), calls=%async_computation.23 | async-start | bytes 3342336 | tf_op jit(solution)/shard_map/reduce_scatter | solution.py:172
  560.2 9.4 copy-start.7
  560.2 405.2 %reduce-scatter.30.cloned.1.call-start = ((), (), s32[]{:S(2)}) async-start(), calls=%async_computation.24 | async-start | bytes 3342336 | tf_op jit(solution)/shard_map/reduce_scatter | solution.py:173
  569.3 524.1 %reduce-scatter.26.cloned.1.call-start = ((), (), s32[]{:S(2)}) async-start(), calls=%async_computation.22 | async-start | bytes 1253376 | tf_op jit(solution)/shard_map/reduce_scatter | solution.py:244
  574.8 646.5 %reduce-scatter.24.cloned.1.call-start = ((), (), s32[]{:S(2)}) async-start(), calls=%async_computation.21 | async-start | bytes 1253376 | tf_op jit(solution)/shard_map/reduce_scatter | solution.py:243
  580.5 768.6 %reduce-scatter.20.cloned.1.call-start = ((), (), s32[]{:S(2)}) async-start(), calls=%async_computation.19 | async-start | bytes 1253376 | tf_op jit(solution)/shard_map/reduce_scatter | solution.py:241
  585.7 5.9 copy-start.5
  585.7 5.9 copy-start.23
  585.7 5.9 copy-start.25
  585.7 891.1 %reduce-scatter.22.cloned.1.call-start = ((), (), s32[]{:S(2)}) async-start(), calls=%async_computation.20 | async-start | bytes 1253376 | tf_op jit(solution)/shard_map/reduce_scatter | solution.py:242
  591.5 49.6 %copy-start.26 = (f32[1152]{0:T(1024)S(1)}, f32[1152]{0:T(1024)}, u32[]{:S(2)}) copy-start(f32[1152]{0:T(1024)} %get-tuple-element.327) | copy-start | bytes 13828
  641.1 835.6 %copy-start.1 = (bf16[1024,768]{1,0:T(8,128)(2,1)S(1)}, bf16[1024,768]{1,0:T(8,128)(2,1)}, u32[]{:S(2)}) copy-start(bf16[1024,768]{1,0:T(8,128)(2,1)} %param.26) | copy-start | bytes 4718596
  (24 other events, 63.0 us)
Sparse Core Ops, SparseCore 0:
  13.7 15.3 all-gather.4
  119.0 16.6 reduce-scatter.11
  141.7 13.8 all-gather.6
  157.1 13.8 all-gather.8
  200.9 16.5 reduce-scatter.15
  219.6 12.6 reduce-scatter.13
  238.3 13.8 all-gather.10
  540.2 16.7 reduce-scatter.17
  562.5 131.8 reduce-scatter.31
  699.8 129.9 reduce-scatter.27
  835.4 129.9 reduce-scatter.29
  970.6 122.7 reduce-scatter.25
  1098.7 122.5 reduce-scatter.23
  1226.4 122.5 reduce-scatter.19
  1354.2 122.5 reduce-scatter.21
